TPU v7x, 32 devices: a whole 2x2x4 slice. The times are simulated.
32 devices in a mesh: dp: 8 (over y, x, core), tensor: 4 (over z).
Axes of the slice: x: 2, y: 2, z: 4, core: 2. Of those that a mesh axis runs over, the one named last changes fastest.
Arguments:
- tokens: bfloat16 [8, 736, 1152], P('dp', 'tensor'), may hold values from -45 to 45
- key_mask: int32 [8, 736], P('dp'), may hold values from 0 to 1, as said below
- query_weight: bfloat16 [1152, 1152], P('dp', 'tensor'), may hold values from -0.1875 to 0.1875
- key_weight: bfloat16 [1152, 1152], P('dp', 'tensor'), may hold values from -0.1875 to 0.1875
- value_weight: bfloat16 [1152, 1152], P('dp', 'tensor'), may hold values from -0.1875 to 0.1875
- out_weight: bfloat16 [1152, 1152], P('tensor', 'dp'), may hold values from -0.375 to 0.375
- up_weight: bfloat16 [1152, 4304], P('dp', 'tensor'), may hold values from -0.1875 to 0.1875
- down_weight: bfloat16 [4304, 1152], P('tensor', 'dp'), may hold values from -0.09375 to 0.09375
- first_gain: bfloat16 [1152], P('dp'), may hold values from 0.5 to 1.5
- first_shift: bfloat16 [1152], P('dp'), may hold values from -3 to 3
- query_bias: bfloat16 [1152], P('dp'), may hold values from -3 to 3
- value_bias: bfloat16 [1152], P('dp'), may hold values from -3 to 3
- out_bias: bfloat16 [1152], P('dp'), may hold values from -3 to 3
- second_gain: bfloat16 [1152], P('dp'), may hold values from 0.5 to 1.5
- second_shift: bfloat16 [1152], P('dp'), may hold values from -3 to 3
- up_bias: bfloat16 [4304], P('dp'), may hold values from -3 to 3
- down_bias: bfloat16 [1152], P('dp'), may hold values from -3 to 3
- cotangent: bfloat16 [8, 736, 1152], P('dp', 'tensor'), may hold values from -6 to 6
Outputs:
- output: bfloat16 [8, 736, 1152], P('dp', 'tensor')
- input_grad: float32 [8, 736, 1152], P('dp', 'tensor')
- query_grad: float32 [1152, 1152], P('dp', 'tensor')
- key_grad: float32 [1152, 1152], P('dp', 'tensor')
- value_grad: float32 [1152, 1152], P('dp', 'tensor')
- out_grad: float32 [1152, 1152], P('tensor', 'dp')
- up_grad: float32 [1152, 4304], P('dp', 'tensor')
- down_grad: float32 [4304, 1152], P('tensor', 'dp')
- first_gain_grad: float32 [1152], P('dp')
- first_shift_grad: float32 [1152], P('dp')
- query_bias_grad: float32 [1152], P('dp')
- value_bias_grad: float32 [1152], P('dp')
- out_bias_grad: float32 [1152], P('dp')
- second_gain_grad: float32 [1152], P('dp')
- second_shift_grad: float32 [1152], P('dp')
- up_bias_grad: float32 [4304], P('dp')
- down_bias_grad: float32 [1152], P('dp')
Inputs may be any that keep to these rules, and one draw needn't show every extreme that they name: `key_mask`: each image's ones form a prefix of its positions, at least its first three quarters.
All inputs are finite; a program needn't handle non-finite values.
Results may differ from a plain program's by a relative error of at most 0.017.
The roundings to bfloat16 on the way count: a program that leaves them out, or rounds other values in their place, can miss the bound.
Values may be sent and summed in bfloat16 or wider, within the bound.
A program may use at most 128 MiB of HBM per device.

v0:
```python
from functools import partial
import math
import jax
import jax.numpy as jnp
from jax import lax
from jax.sharding import PartitionSpec as P

HD = 72
EPSILON = 1e-06
GELU_COEF = 0.7978845608028654
MASK_FILL = -1e30


def norm_forward(inputs, gain_vec, shift_vec):
    centred = inputs - jnp.mean(inputs, axis=-1, keepdims=True)
    inv_std = lax.rsqrt(jnp.mean(centred * centred, axis=-1, keepdims=True) + EPSILON)
    normed = centred * inv_std
    return (normed * gain_vec + shift_vec, normed, inv_std)


def norm_backward(grad_in, normed, inv_std, gain_vec):
    scaled = grad_in * gain_vec
    return inv_std * (
        scaled
        - jnp.mean(scaled, axis=-1, keepdims=True)
        - normed * jnp.mean(scaled * normed, axis=-1, keepdims=True)
    )


def gelu_pair(pre_act):
    tanh_val = jnp.tanh(GELU_COEF * (pre_act + 0.044715 * pre_act * pre_act * pre_act))
    gelu_value = 0.5 * pre_act * (1.0 + tanh_val)
    gelu_slope = 0.5 * (1.0 + tanh_val) + 0.5 * pre_act * (
        1.0 - tanh_val * tanh_val
    ) * GELU_COEF * (1.0 + 3.0 * 0.044715 * pre_act * pre_act)
    return (gelu_value, gelu_slope)


def mat_dot(left, right):
    return jnp.dot(left, right, preferred_element_type=jnp.float32)


def gather_rows(local):
    return lax.all_gather(local, "tensor", axis=1, tiled=True)


def sum_rows(partial_term):
    return lax.psum_scatter(
        partial_term.astype(jnp.bfloat16), "tensor", scatter_dimension=1, tiled=True
    ).astype(jnp.float32)


def attend_image(packed):
    query_img, keys_img, values_img, valid_img = packed
    scores = jnp.einsum("qhd,khd->hqk", query_img, keys_img, preferred_element_type=jnp.float32)
    scores = jnp.where(valid_img[None, None, :] > 0, scores, MASK_FILL)
    highest = jnp.max(scores, axis=-1, keepdims=True)
    logsum = highest + jnp.log(jnp.sum(jnp.exp(scores - highest), axis=-1, keepdims=True))
    probs = jnp.exp(scores - logsum).astype(jnp.bfloat16)
    mixed = jnp.einsum("hqk,khd->qhd", probs, values_img, preferred_element_type=jnp.float32)
    return (mixed.astype(jnp.bfloat16), logsum[..., 0])


def attend_back(scale_factor, packed):
    query_img, keys_img, values_img, valid_img, logsum_img, mixed_img, grad_img = packed
    scores = jnp.einsum("qhd,khd->hqk", query_img, keys_img, preferred_element_type=jnp.float32)
    scores = jnp.where(valid_img[None, None, :] > 0, scores, MASK_FILL)
    probs_full = jnp.exp(scores - logsum_img[:, :, None])
    probs = probs_full.astype(jnp.bfloat16)
    grad_values = jnp.einsum("hqk,qhd->khd", probs, grad_img, preferred_element_type=jnp.float32)
    grad_probs = jnp.einsum(
        "qhd,khd->hqk", grad_img, values_img, preferred_element_type=jnp.float32
    )
    delta = jnp.sum(grad_img.astype(jnp.float32) * mixed_img.astype(jnp.float32), axis=-1).T
    grad_scores = (probs_full * (grad_probs - delta[:, :, None])).astype(jnp.bfloat16)
    grad_query = (
        jnp.einsum("hqk,khd->qhd", grad_scores, keys_img, preferred_element_type=jnp.float32)
        * scale_factor
    )
    grad_keys = jnp.einsum(
        "hqk,qhd->khd", grad_scores, query_img, preferred_element_type=jnp.float32
    )
    return (grad_query, grad_keys, grad_values)


def vector_share(full_vec, parts, index):
    piece = full_vec.shape[0] // parts
    return lax.dynamic_slice_in_dim(full_vec, index * piece, piece)


def shards(
    tokens,
    key_mask,
    query_weight,
    key_weight,
    value_weight,
    out_weight,
    up_weight,
    down_weight,
    first_gain,
    first_shift,
    query_bias,
    value_bias,
    out_bias,
    second_gain,
    second_shift,
    up_bias,
    down_bias,
    cotangent,
):
    dp_count = lax.axis_size("dp")
    dp_index = lax.axis_index("dp")
    tensor_index = lax.axis_index("tensor")
    images = tokens.shape[0]
    width = tokens.shape[2]
    fetched = (
        lax.all_gather(query_weight, "dp", axis=0, tiled=True),
        lax.all_gather(key_weight, "dp", axis=0, tiled=True),
        lax.all_gather(value_weight, "dp", axis=0, tiled=True),
        lax.all_gather(out_weight, "dp", axis=1, tiled=True),
        lax.all_gather(up_weight, "dp", axis=0, tiled=True),
        lax.all_gather(down_weight, "dp", axis=1, tiled=True),
        lax.all_gather(first_gain, "dp", axis=0, tiled=True),
        lax.all_gather(first_shift, "dp", axis=0, tiled=True),
        lax.all_gather(query_bias, "dp", axis=0, tiled=True),
        lax.all_gather(value_bias, "dp", axis=0, tiled=True),
        lax.all_gather(out_bias, "dp", axis=0, tiled=True),
        lax.all_gather(second_gain, "dp", axis=0, tiled=True),
        lax.all_gather(second_shift, "dp", axis=0, tiled=True),
        lax.all_gather(up_bias, "dp", axis=0, tiled=True),
        lax.all_gather(down_bias, "dp", axis=0, tiled=True),
    )
    query_full, key_full, value_full, out_full, up_full, down_full = fetched[:6]
    (
        gain_one,
        shift_one,
        query_bias_all,
        value_bias_all,
        out_bias_all,
        gain_two,
        shift_two,
        up_bias_all,
        down_bias_all,
    ) = [member.astype(jnp.float32) for member in fetched[6:]]
    head_cols = query_full.shape[1]
    hidden_cols = up_full.shape[1]
    heads_local = head_cols // HD
    query_bias_local = lax.dynamic_slice_in_dim(query_bias_all, tensor_index * head_cols, head_cols)
    value_bias_local = lax.dynamic_slice_in_dim(value_bias_all, tensor_index * head_cols, head_cols)
    up_bias_local = lax.dynamic_slice_in_dim(up_bias_all, tensor_index * hidden_cols, hidden_cols)
    scale_factor = 1.0 / math.sqrt(HD)
    inputs = tokens.astype(jnp.float32)
    first, normed_one, inv_one = norm_forward(inputs, gain_one, shift_one)
    first_rows = gather_rows(first.astype(jnp.bfloat16))
    seq_full = first_rows.shape[1]
    row_shape = (images, seq_full, width)
    head_shape = (images, seq_full, heads_local, HD)
    first_flat = first_rows.reshape(-1, width)
    query = (
        ((mat_dot(first_flat, query_full) + query_bias_local) * scale_factor)
        .astype(jnp.bfloat16)
        .reshape(head_shape)
    )
    keys = mat_dot(first_flat, key_full).astype(jnp.bfloat16).reshape(head_shape)
    values = (
        (mat_dot(first_flat, value_full) + value_bias_local)
        .astype(jnp.bfloat16)
        .reshape(head_shape)
    )
    mixed, logsum = lax.map(attend_image, (query, keys, values, key_mask))
    mixed_flat = mixed.reshape(-1, head_cols)
    hidden = inputs + sum_rows(mat_dot(mixed_flat, out_full).reshape(row_shape)) + out_bias_all
    second, normed_two, inv_two = norm_forward(hidden, gain_two, shift_two)
    second_flat = gather_rows(second.astype(jnp.bfloat16)).reshape(-1, width)
    pre_act = mat_dot(second_flat, up_full) + up_bias_local
    gelu_value, gelu_slope = gelu_pair(pre_act)
    act = gelu_value.astype(jnp.bfloat16)
    output = (hidden + sum_rows(mat_dot(act, down_full).reshape(row_shape)) + down_bias_all).astype(
        jnp.bfloat16
    )
    query_back, key_back, value_back, out_back, up_back, down_back = (
        lax.all_gather(query_weight, "dp", axis=0, tiled=True),
        lax.all_gather(key_weight, "dp", axis=0, tiled=True),
        lax.all_gather(value_weight, "dp", axis=0, tiled=True),
        lax.all_gather(out_weight, "dp", axis=1, tiled=True),
        lax.all_gather(up_weight, "dp", axis=0, tiled=True),
        lax.all_gather(down_weight, "dp", axis=1, tiled=True),
    )
    grad_out = cotangent.astype(jnp.float32)
    down_bias_grad = jnp.sum(grad_out, axis=(0, 1))
    grad_rows = gather_rows(cotangent).reshape(-1, width)
    down_grad = mat_dot(act.T, grad_rows)
    grad_pre = mat_dot(grad_rows, down_back.T) * gelu_slope
    up_bias_part = jnp.sum(grad_pre, axis=0)
    grad_pre_low = grad_pre.astype(jnp.bfloat16)
    up_grad = mat_dot(second_flat.T, grad_pre_low)
    grad_second = sum_rows(mat_dot(grad_pre_low, up_back.T).reshape(row_shape))
    second_gain_grad = jnp.sum(grad_second * normed_two, axis=(0, 1))
    second_shift_grad = jnp.sum(grad_second, axis=(0, 1))
    grad_hidden = grad_out + norm_backward(grad_second, normed_two, inv_two, gain_two)
    out_bias_grad = jnp.sum(grad_hidden, axis=(0, 1))
    hidden_rows = gather_rows(grad_hidden.astype(jnp.bfloat16)).reshape(-1, width)
    grad_mixed = mat_dot(hidden_rows, out_back.T).astype(jnp.bfloat16)
    out_grad = mat_dot(mixed_flat.T, hidden_rows)
    grad_query_f, grad_keys_f, grad_values_f = lax.map(
        partial(attend_back, scale_factor),
        (query, keys, values, key_mask, logsum, mixed, grad_mixed.reshape(head_shape)),
    )
    grad_query_f = grad_query_f.reshape(-1, head_cols)
    grad_keys_f = grad_keys_f.reshape(-1, head_cols)
    grad_values_f = grad_values_f.reshape(-1, head_cols)
    query_bias_part = jnp.sum(grad_query_f, axis=0)
    value_bias_part = jnp.sum(grad_values_f, axis=0)
    grad_query = grad_query_f.astype(jnp.bfloat16)
    grad_keys = grad_keys_f.astype(jnp.bfloat16)
    grad_values = grad_values_f.astype(jnp.bfloat16)
    query_grad = mat_dot(first_flat.T, grad_query)
    key_grad = mat_dot(first_flat.T, grad_keys)
    value_grad = mat_dot(first_flat.T, grad_values)
    first_term = (
        mat_dot(grad_query, query_back.T)
        + mat_dot(grad_keys, key_back.T)
        + mat_dot(grad_values, value_back.T)
    )
    grad_first = sum_rows(first_term.reshape(row_shape))
    first_gain_grad = jnp.sum(grad_first * normed_one, axis=(0, 1))
    first_shift_grad = jnp.sum(grad_first, axis=(0, 1))
    input_grad = grad_hidden + norm_backward(grad_first, normed_one, inv_one, gain_one)
    matrix_shares = (
        lax.psum_scatter(query_grad, "dp", scatter_dimension=0, tiled=True),
        lax.psum_scatter(key_grad, "dp", scatter_dimension=0, tiled=True),
        lax.psum_scatter(value_grad, "dp", scatter_dimension=0, tiled=True),
        lax.psum_scatter(out_grad, "dp", scatter_dimension=1, tiled=True),
        lax.psum_scatter(up_grad, "dp", scatter_dimension=0, tiled=True),
        lax.psum_scatter(down_grad, "dp", scatter_dimension=1, tiled=True),
    )
    query_bias_full = lax.dynamic_update_slice_in_dim(
        jnp.zeros((width,), jnp.float32), query_bias_part, tensor_index * head_cols, 0
    )
    value_bias_full = lax.dynamic_update_slice_in_dim(
        jnp.zeros((width,), jnp.float32), value_bias_part, tensor_index * head_cols, 0
    )
    up_bias_full = lax.dynamic_update_slice_in_dim(
        jnp.zeros((up_bias_all.shape[0],), jnp.float32), up_bias_part, tensor_index * hidden_cols, 0
    )
    vector_sums = lax.psum(
        (
            first_gain_grad,
            first_shift_grad,
            query_bias_full,
            value_bias_full,
            out_bias_grad,
            second_gain_grad,
            second_shift_grad,
            up_bias_full,
            down_bias_grad,
        ),
        ("dp", "tensor"),
    )
    vector_parts = tuple((vector_share(member, dp_count, dp_index) for member in vector_sums))
    return (output, input_grad) + tuple(matrix_shares) + vector_parts


def solution(mesh):
    return jax.shard_map(
        shards,
        mesh=mesh,
        in_specs=(
            P("dp", "tensor", None),
            P("dp", None),
            P("dp", "tensor"),
            P("dp", "tensor"),
            P("dp", "tensor"),
            P("tensor", "dp"),
            P("dp", "tensor"),
            P("tensor", "dp"),
            P("dp"),
            P("dp"),
            P("dp"),
            P("dp"),
            P("dp"),
            P("dp"),
            P("dp"),
            P("dp"),
            P("dp"),
            P("dp", "tensor", None),
        ),
        out_specs=(
            P("dp", "tensor", None),
            P("dp", "tensor", None),
            P("dp", "tensor"),
            P("dp", "tensor"),
            P("dp", "tensor"),
            P("tensor", "dp"),
            P("dp", "tensor"),
            P("tensor", "dp"),
            P("dp"),
            P("dp"),
            P("dp"),
            P("dp"),
            P("dp"),
            P("dp"),
            P("dp"),
            P("dp"),
            P("dp"),
        ),
        check_vma=False,
    )
```

profile of v0, /device:TPU:0, one launch (start us, length us, event | category | flops | bytes accessed | tf_op | source)
XLA Modules:
  0.0 748.6 jit_solution(14068338893583376241)
XLA Ops:
  20.8 26.1 %all-reduce.14 = (bf16[1152]{0:T(1024)(128)(2,1)S(1)}, bf16[1152]{0:T(1024)(128)(2,1)S(1)}, bf16[1152]{0:T(1024)(128)(2,1)S(1)}, bf16[1152]{0:T(1024)(128)(2,1)S...) all-reduce(bf16[1152]{0:T(1024)(128)(2,1)S(1)} %dynamic-update-slic, ...), channel_id=1, replica_groups=mesh['dp'=8,'tensor'=4] {'dp'}, use_global_device_ids=true, to_apply=%add.6 | all-reduce | flops 13520 | bytes 54080
  49.9 10.0 %all_gather.68 = bf16[1152,288]{1,0:T(8,128)(2,1)S(1)} all-gather(bf16[144,288]{1,0:T(8,128)(2,1)} %param.20), channel_id=1, replica_groups=mesh['dp'=8,'tensor'=4] {'dp'}, dimensions={0}, use_global_device_ids=true | all-gather | bytes 746496 | tf_op jit(solution)/shard_map/all_gather | solution.py:117
  59.9 10.5 %all_gather.70 = bf16[1152,288]{1,0:T(8,128)(2,1)S(1)} all-gather(bf16[144,288]{1,0:T(8,128)(2,1)S(1)} %copy-done.18), channel_id=1, replica_groups=mesh['dp'=8,'tensor'=4] {'dp'}, dimensions={0}, use_global_device_ids=true | all-gather | bytes 746496 | tf_op jit(solution)/shard_map/all_gather | solution.py:118
  70.4 10.2 %all_gather.66 = bf16[1152,288]{1,0:T(8,128)(2,1)S(1)} all-gather(bf16[144,288]{1,0:T(8,128)(2,1)S(1)} %copy-done.19), channel_id=1, replica_groups=mesh['dp'=8,'tensor'=4] {'dp'}, dimensions={0}, use_global_device_ids=true | all-gather | bytes 746496 | tf_op jit(solution)/shard_map/all_gather | solution.py:119
  80.5 11.5 %all_gather.71 = bf16[288,1152]{0,1:T(8,128)(2,1)} all-gather(bf16[288,144]{0,1:T(8,128)(2,1)S(1)} %copy-done.20), channel_id=1, replica_groups=mesh['dp'=8,'tensor'=4] {'dp'}, dimensions={1}, use_global_device_ids=true | all-gather | bytes 746496 | tf_op jit(solution)/shard_map/all_gather | solution.py:120
  106.2 37.0 %reduce-scatter.35.cloned.1.call-done = bf16[1,184,1152]{2,1,0:T(8,128)(2,1)} async-done(((bf16[1,736,1152]{2,1,0:T(8,128)(2,1)}), bf16[1,184,1152]{2,1,0:T(8,128)(2,1)}) %reduce-scatter.35.cloned.1.call-update) | async-done | bytes 423952
  149.5 36.8 %all-gather.9.cloned.1.call-done = bf16[1,736,1152]{2,1,0:T(8,128)(2,1)} async-done(((bf16[1,184,1152]{2,1,0:T(8,128)(2,1)}), bf16[1,736,1152]{2,1,0:T(8,128)(2,1)}) %all-gather.9.cloned.1.call-update) | async-done | bytes 1695760 | tf_op jit(solution)/shard_map/all_gather | solution.py:44
  186.3 6.4 convolution_add_fusion.2
  192.8 32.8 %all-gather.15.cloned.1.call-done = bf16[1,736,1152]{2,1,0:T(8,128)(2,1)} async-done(((bf16[1,184,1152]{2,1,0:T(8,128)(2,1)}), bf16[1,736,1152]{2,1,0:T(8,128)(2,1)}) %all-gather.15.cloned.1.call-update) | async-done | bytes 1695760 | tf_op jit(solution)/shard_map/all_gather | solution.py:44
  225.6 30.9 %all-gather.13.cloned.1.call-done = bf16[1076,1152]{0,1:T(8,128)(2,1)} async-done(((bf16[1076,144]{0,1:T(8,128)(2,1)}), bf16[1076,1152]{0,1:T(8,128)(2,1)}) %all-gather.13.cloned.1.call-update) | async-done | bytes 2479120 | tf_op jit(solution)/shard_map/all_gather | solution.py:122
  256.5 8.2 %fusion.86 = (f32[1076]{0:T(1024)}, bf16[736,1076]{0,1:T(8,128)(2,1)S(1)}) fusion(f32[736,1076]{0,1:T(8,128)} %convolution_add_fusion.2, bf16[1076,1152]{0,1:T(8,128)(2,1)} %all-gather.13.cloned.1.call-done, bf16[1,736,1152]{2,1,0:T(8,128)(2,1)} %all-gather.15.cloned.1.call-done), kind=kOutput, calls=%fused_computation.117 | convolution fusion | flops 1840458240 | bytes 8930768 | tf_op jit(solution)/shard_map/dot_general | solution.py:40
  265.9 4.0 fusion.8
  269.9 7.2 fusion.7
  277.2 30.1 %reduce-scatter.39.cloned.1.call-done = bf16[1,184,1152]{2,1,0:T(8,128)(2,1)} async-done(((bf16[1,736,1152]{2,1,0:T(8,128)(2,1)}), bf16[1,184,1152]{2,1,0:T(8,128)(2,1)}) %reduce-scatter.39.cloned.1.call-update) | async-done | bytes 423952
  309.5 36.8 %reduce-scatter.37.cloned.1.call-done = bf16[1,184,1152]{2,1,0:T(8,128)(2,1)} async-done(((bf16[1,736,1152]{2,1,0:T(8,128)(2,1)}), bf16[1,184,1152]{2,1,0:T(8,128)(2,1)}) %reduce-scatter.37.cloned.1.call-update) | async-done | bytes 423952
  350.3 38.2 %all-gather.17.cloned.1.call-done = bf16[1,736,1152]{2,1,0:T(8,128)(2,1)} async-done(((bf16[1,184,1152]{2,1,0:T(8,128)(2,1)}), bf16[1,736,1152]{2,1,0:T(8,128)(2,1)}) %all-gather.17.cloned.1.call-update) | async-done | bytes 1695760 | tf_op jit(solution)/shard_map/all_gather | solution.py:44
  392.1 5.6 fusion.84
  397.8 5.6 multiply_convert_fusion
  410.8 7.4 fusion.15
  419.7 6.5 fusion.18
  427.2 3.9 fusion.11
  431.2 3.9 fusion.21
  435.2 3.9 fusion.25
  439.2 3.8 fusion.23
  444.0 2.7 reduce-scatter.41.cloned.1.call-done
  448.2 41.8 %all-reduce.13 = (f32[1152]{0:T(1024)S(1)}, f32[1152]{0:T(1024)S(1)}, f32[1152]{0:T(1024)S(1)}, f32[1152]{0:T(1024)S(1)}, f32[1152]{0:T(1024)S(1)}, /*index=5*/f...) all-reduce(f32[1152]{0:T(1024)S(1)} %get-tuple-element.73, ...), channel_id=1, replica_groups=mesh['dp'=8,'tensor'=4] {'dp','tensor'}, use_global_device_ids=true, to_apply=%region_22.23 | all-reduce | flops 13520 | bytes 108160 | tf_op jit(solution)/shard_map/psum | solution.py:246
  498.0 9.4 %reduce-scatter.33.cloned.1.call-done = f32[1076,144]{0,1:T(8,128)} async-done(((f32[1076,1152]{0,1:T(8,128)}), f32[1076,144]{0,1:T(8,128)}) %reduce-scatter.33.cloned.1.call-update) | async-done | bytes 619792 | tf_op jit(solution)/shard_map/reduce_scatter | solution.py:235
  507.5 61.1 %reduce-scatter.31.cloned.1.call-done = f32[144,1076]{1,0:T(8,128)} async-done(((f32[1152,1076]{1,0:T(8,128)}), f32[144,1076]{1,0:T(8,128)}) %reduce-scatter.31.cloned.1.call-update) | async-done | bytes 619792 | tf_op jit(solution)/shard_map/reduce_scatter | solution.py:234
  568.5 43.1 %reduce-scatter.29.cloned.1.call-done = f32[288,144]{0,1:T(8,128)} async-done(((f32[288,1152]{0,1:T(8,128)}), f32[288,144]{0,1:T(8,128)}) %reduce-scatter.29.cloned.1.call-update) | async-done | bytes 165904 | tf_op jit(solution)/shard_map/reduce_scatter | solution.py:233
  611.6 43.1 %reduce-scatter.27.cloned.1.call-done = f32[144,288]{1,0:T(8,128)} async-done(((f32[1152,288]{1,0:T(8,128)}), f32[144,288]{1,0:T(8,128)}) %reduce-scatter.27.cloned.1.call-update) | async-done | bytes 165904 | tf_op jit(solution)/shard_map/reduce_scatter | solution.py:232
  654.7 43.3 %reduce-scatter.23.cloned.1.call-done = f32[144,288]{1,0:T(8,128)} async-done(((f32[1152,288]{1,0:T(8,128)}), f32[144,288]{1,0:T(8,128)}) %reduce-scatter.23.cloned.1.call-update) | async-done | bytes 165904 | tf_op jit(solution)/shard_map/reduce_scatter | solution.py:230
  698.0 43.1 %reduce-scatter.25.cloned.1.call-done = f32[144,288]{1,0:T(8,128)} async-done(((f32[1152,288]{1,0:T(8,128)}), f32[144,288]{1,0:T(8,128)}) %reduce-scatter.25.cloned.1.call-update) | async-done | bytes 165904 | tf_op jit(solution)/shard_map/reduce_scatter | solution.py:231
  (173 shorter events, 66.2 us)
Async XLA Ops:
  8.0 51.8 %copy-start.18 = (bf16[144,288]{1,0:T(8,128)(2,1)S(1)}, bf16[144,288]{1,0:T(8,128)(2,1)}, u32[]{:S(2)}) copy-start(bf16[144,288]{1,0:T(8,128)(2,1)} %param.21) | copy-start | bytes 248836
  8.0 62.3 %copy-start.19 = (bf16[144,288]{1,0:T(8,128)(2,1)S(1)}, bf16[144,288]{1,0:T(8,128)(2,1)}, u32[]{:S(2)}) copy-start(bf16[144,288]{1,0:T(8,128)(2,1)} %param.22) | copy-start | bytes 248836
  8.0 72.5 %copy-start.20 = (bf16[288,144]{0,1:T(8,128)(2,1)S(1)}, bf16[288,144]{0,1:T(8,128)(2,1)}, u32[]{:S(2)}) copy-start(bf16[288,144]{0,1:T(8,128)(2,1)} %param.23) | copy-start | bytes 248836
  8.1 84.0 %all-gather.7.cloned.1.call-start = ((), (), s32[]{:S(2)}) async-start(), calls=%async_computation.10 | async-start | bytes 2119680 | tf_op jit(solution)/shard_map/all_gather | solution.py:44
  48.9 94.3 %reduce-scatter.35.cloned.1.call-start = ((), (), s32[]{:S(2)}) async-start(), calls=%async_computation.22 | async-start | bytes 2119680
  70.4 24.9 %copy-start.3 = (bf16[1152,288]{1,0:T(8,128)(2,1)}, bf16[1152,288]{1,0:T(8,128)(2,1)S(1)}, u32[]{:S(2)}) copy-start(bf16[1152,288]{1,0:T(8,128)(2,1)S(1)} %all_gather.70) | copy-start | bytes 1990660
  98.8 3.5 copy-start.21
  102.3 40.9 %copy-start = (bf16[1,184,1152]{2,1,0:T(8,128)(2,1)S(1)}, bf16[1,184,1152]{2,1,0:T(8,128)(2,1)}, u32[]{:S(2)}) copy-start(bf16[1,184,1152]{2,1,0:T(8,128)(2,1)} %param.18) | copy-start | bytes 1271812
  105.5 44.0 %all-gather.11.cloned.1.call-start = ((), (), s32[]{:S(2)}) async-start(), calls=%async_computation.12 | async-start | bytes 2985984 | tf_op jit(solution)/shard_map/all_gather | solution.py:121
  106.1 80.2 %all-gather.9.cloned.1.call-start = ((), (), s32[]{:S(2)}) async-start(), calls=%async_computation.11 | async-start | bytes 2119680 | tf_op jit(solution)/shard_map/all_gather | solution.py:44
  147.8 77.8 %all-gather.15.cloned.1.call-start = ((), (), s32[]{:S(2)}) async-start(), calls=%async_computation.14 | async-start | bytes 2119680 | tf_op jit(solution)/shard_map/all_gather | solution.py:44
  148.4 108.1 %all-gather.13.cloned.1.call-start = ((), (), s32[]{:S(2)}) async-start(), calls=%async_computation.13 | async-start | bytes 2985984 | tf_op jit(solution)/shard_map/all_gather | solution.py:122
  149.1 158.2 %reduce-scatter.39.cloned.1.call-start = ((), (), s32[]{:S(2)}) async-start(), calls=%async_computation.24 | async-start | bytes 2119680
  256.5 9.4 %copy-start.24 = (bf16[1152,1076]{1,0:T(8,128)(2,1)S(1)}, bf16[1152,1076]{1,0:T(8,128)(2,1)}, u32[]{:S(2)}) copy-start(bf16[1152,1076]{1,0:T(8,128)(2,1)} %all-gather.11.cloned.1.call-done) | copy-start | bytes 7437316
  269.9 37.4 %copy-start.2 = (bf16[1,184,1152]{2,1,0:T(8,128)(2,1)S(1)}, bf16[1,184,1152]{2,1,0:T(8,128)(2,1)}, u32[]{:S(2)}) copy-start(bf16[1,184,1152]{2,1,0:T(8,128)(2,1)} %reduce-scatter.35.cloned.1.call-done) | copy-start | bytes 1271812
  269.9 76.4 %reduce-scatter.37.cloned.1.call-start = ((), (), s32[]{:S(2)}) async-start(), calls=%async_computation.23 | async-start | bytes 2119680
  277.2 111.3 %all-gather.17.cloned.1.call-start = ((), (), s32[]{:S(2)}) async-start(), calls=%async_computation.15 | async-start | bytes 2119680 | tf_op jit(solution)/shard_map/all_gather | solution.py:44
  348.9 43.2 %copy-start.22 = (f32[4,736]{1,0:T(4,128)S(1)}, f32[4,736]{1,0:T(4,128)}, u32[]{:S(2)}) copy-start(f32[4,736]{1,0:T(4,128)} %copy-done.21) | copy-start | bytes 35332
  349.8 96.9 %reduce-scatter.41.cloned.1.call-start = ((), (), s32[]{:S(2)}) async-start(), calls=%async_computation.25 | async-start | bytes 2119680
  392.1 5.7 copy-start.28
  397.8 10.6 %copy-start.14 = (bf16[736,4,72]{0,2,1:T(8,128)(2,1)}, bf16[736,4,72]{0,2,1:T(8,128)(2,1)S(1)}, u32[]{:S(2)}) copy-start(bf16[736,4,72]{0,2,1:T(8,128)(2,1)S(1)} %get-tuple-element.100) | copy-start | bytes 1271812
  397.8 5.6 copy-start.10
  410.8 96.7 %reduce-scatter.33.cloned.1.call-start = ((), (), s32[]{:S(2)}) async-start(), calls=%async_computation.21 | async-start | bytes 5971968 | tf_op jit(solution)/shard_map/reduce_scatter | solution.py:235
  418.2 150.3 %reduce-scatter.31.cloned.1.call-start = ((), (), s32[]{:S(2)}) async-start(), calls=%async_computation.20 | async-start | bytes 5971968 | tf_op jit(solution)/shard_map/reduce_scatter | solution.py:234
  426.2 5.0 copy-start.15
  426.2 185.4 %reduce-scatter.29.cloned.1.call-start = ((), (), s32[]{:S(2)}) async-start(), calls=%async_computation.19 | async-start | bytes 1990656 | tf_op jit(solution)/shard_map/reduce_scatter | solution.py:233
  431.1 4.1 copy-start.6
  431.1 223.6 %reduce-scatter.27.cloned.1.call-start = ((), (), s32[]{:S(2)}) async-start(), calls=%async_computation.18 | async-start | bytes 1990656 | tf_op jit(solution)/shard_map/reduce_scatter | solution.py:232
  435.1 4.1 copy-start.12
  435.1 262.8 %reduce-scatter.23.cloned.1.call-start = ((), (), s32[]{:S(2)}) async-start(), calls=%async_computation.16 | async-start | bytes 1990656 | tf_op jit(solution)/shard_map/reduce_scatter | solution.py:230
  439.1 3.9 copy-start.23
  439.1 302.0 %reduce-scatter.25.cloned.1.call-start = ((), (), s32[]{:S(2)}) async-start(), calls=%async_computation.17 | async-start | bytes 1990656 | tf_op jit(solution)/shard_map/reduce_scatter | solution.py:231
  (14 other events, 26.0 us)
Sparse Core Ops, SparseCore 0:
  49.1 38.4 all-gather.6
  105.7 37.5 reduce-scatter.34
  270.0 37.2 reduce-scatter.38
  309.5 36.7 reduce-scatter.36
  349.9 38.5 all-gather.16
Sparse Core Ops, SparseCore 1:
  107.9 30.3 all-gather.10
  147.9 38.4 all-gather.8
  187.8 37.8 all-gather.14
  227.5 28.9 all-gather.12
  410.9 35.8 reduce-scatter.40
  450.7 56.7 reduce-scatter.32
  511.7 56.8 reduce-scatter.30
  572.3 39.2 reduce-scatter.28
  615.4 39.2 reduce-scatter.26
  658.7 39.2 reduce-scatter.22
  701.8 39.2 reduce-scatter.24
where the time goes:
time: 754 us; the launch traced here: 749 us
  waiting for transfers between devices  490 us (65%)
  blocking collectives  110 us (15%)
  matrix products  86 us (11%)
  other arithmetic  22.3 us (3%)
  local copies, waits for them, and re-layouts  20.8 us (3%)
  between operations  17.6 us (2%)
    unnamed x20, waiting for transfers between devices  109 us
    all_gather x4, waiting for transfers between devices, gather_rows(): return lax.all_gather(local, 'tensor', axis=1, tiled=True)  108 us
    dot_general x18, matrix products, mat_dot(): return jnp.dot(left, right, preferred_element_type=jnp.float32)  68.7 us
    reduce_scatter x1, waiting for transfers between devices, shards(): lax.psum_scatter(up_grad, 'dp', scatter_dimension=0, tiled=True)  61.1 us
    reduce_scatter x1, waiting for transfers between devices, shards(): lax.psum_scatter(query_grad, 'dp', scatter_dimension=0, tiled=True)  43.3 us
    reduce_scatter x1, waiting for transfers between devices, shards(): lax.psum_scatter(key_grad, 'dp', scatter_dimension=0, tiled=True)  43.1 us
    reduce_scatter x1, waiting for transfers between devices, shards(): lax.psum_scatter(value_grad, 'dp', scatter_dimension=0, tiled=True)  43.1 us
    reduce_scatter x1, waiting for transfers between devices, shards(): lax.psum_scatter(out_grad, 'dp', scatter_dimension=1, tiled=True)  43.1 us
  transfers between devices with their start and end apart: 16, of which 14 were waited for; matrix products, arithmetic and copies ran while one was open for 8% of the time, Pallas kernels for 0%

commit v1 on v0

--- a/solution.py
+++ b/solution.py
@@ -1,3 +1,4 @@
+import functools
 from functools import partial
 import math
 import jax
@@ -9,6 +10,28 @@
 EPSILON = 1e-06
 GELU_COEF = 0.7978845608028654
 MASK_FILL = -1e30
+
+
+def trees_switch(a0, shard_axis):
+    shaped, response, z = (
+        jax.lax.axis_size(shard_axis),
+        jax.lax.axis_index(shard_axis),
+        a0.shape[1],
+    )
+    x_next, u1 = (a0, 1)
+    while u1 < shaped:
+        so_far_all = []
+        for dev_i in tuple(range(shaped)):
+            so_far_all.append((dev_i, (dev_i - u1) % shaped))
+        x_next = jnp.concatenate(
+            [x_next, jax.lax.ppermute(x_next, axis_name=shard_axis, perm=so_far_all)], 1
+        )
+        u1 = 2 * u1
+    u_next = jnp.roll(x_next, response * z, axis=1)
+    return u_next
+
+
+write_ends_here = functools.partial(trees_switch, shard_axis="tensor")
 
 
 def norm_forward(inputs, gain_vec, shift_vec):
@@ -41,7 +64,7 @@
 
 
 def gather_rows(local):
-    return lax.all_gather(local, "tensor", axis=1, tiled=True)
+    return write_ends_here(local)
 
 
 def sum_rows(partial_term):

time: 754 us -> 795 us (1.054)
  other arithmetic: 22.3 us -> 48.3 us
  starting transfers between devices: 1.54 us -> 15.7 us
    ppermute x0 -> x8, waiting for transfers between devices: none -> 126 us  [trees_switch(): jax.lax.ppermute(x_next, axis_name=shard_axis, perm=so_far_all)]
    all_gather x4 -> x0, waiting for transfers between devices: 108 us -> none  [gather_rows(): return lax.all_gather(local, 'tensor', axis=1, tiled=True)]
    reduce_scatter x1, waiting for transfers between devices: 9.44 us -> 60.9 us  [shards(): lax.psum_scatter(down_grad, 'dp', scatter_dimension=1, tiled=True)]
    reduce_scatter x1, waiting for transfers between devices: 43.1 us -> 0.01 us  [shards(): lax.psum_scatter(out_grad, 'dp', scatter_dimension=1, tiled=True)]
    all_gather x1, waiting for transfers between devices: 30.9 us -> 0.01 us  [shards(): lax.all_gather(down_weight, 'dp', axis=1, tiled=True)]
    reshape x0 -> x4, other arithmetic: none -> 27.8 us  [the longest x1 7.42 us: shards(): grad_rows = gather_rows(cotangent).reshape(-1, width)]
    ppermute x0 -> x8, starting transfers between devices: none -> 14.8 us  [trees_switch(): jax.lax.ppermute(x_next, axis_name=shard_axis, perm=so_far_all)]
    dot_general x1, matrix products: 1.86 us -> 12.8 us  [attend_image(): jnp.einsum('hqk,khd->qhd', probs, values_img, preferred_element_type=jnp....]
  transfers between devices with their start and end apart: 16 -> 20, of which waited for: 14 -> 15; matrix products, arithmetic and copies ran while one was open for 8% -> 10% of each run, Pallas kernels for 0% -> 0%
where the time goes in v1:
time: 795 us; the launch traced here: 789 us
  waiting for transfers between devices  484 us (61%)
  blocking collectives  111 us (14%)
  matrix products  91.4 us (11%)
  other arithmetic  48.3 us (6%)
  local copies, waits for them, and re-layouts  21.5 us (3%)
  between operations  17.8 us (2%)
  starting transfers between devices  15.7 us (2%)
    ppermute x8, waiting for transfers between devices, trees_switch(): jax.lax.ppermute(x_next, axis_name=shard_axis, perm=so_far_all)  126 us
    unnamed x16, waiting for transfers between devices  114 us
    dot_general x18, matrix products, mat_dot(): return jnp.dot(left, right, preferred_element_type=jnp.float32)  65.3 us
    reduce_scatter x1, waiting for transfers between devices, shards(): lax.psum_scatter(up_grad, 'dp', scatter_dimension=0, tiled=True)  61.2 us
    reduce_scatter x1, waiting for transfers between devices, shards(): lax.psum_scatter(down_grad, 'dp', scatter_dimension=1, tiled=True)  60.9 us
    reduce_scatter x1, waiting for transfers between devices, shards(): lax.psum_scatter(query_grad, 'dp', scatter_dimension=0, tiled=True)  43.4 us
    reduce_scatter x1, waiting for transfers between devices, shards(): lax.psum_scatter(key_grad, 'dp', scatter_dimension=0, tiled=True)  43.4 us
    psum x1, blocking collectives, shards(): lax.psum((first_gain_grad, first_shift_grad, query_bias_full, value_bias_...  41.7 us
  transfers between devices with their start and end apart: 20, of which 15 were waited for; matrix products, arithmetic and copies ran while one was open for 10% of the time, Pallas kernels for 0%

profile of v1, /device:TPU:0, one launch (start us, length us, event | category | flops | bytes accessed | tf_op | source)
XLA Modules:
  0.0 789.0 jit_solution(2423756653553187605)
XLA Ops:
  20.9 26.1 %all-reduce.14 = (bf16[1152]{0:T(1024)(128)(2,1)S(1)}, bf16[1152]{0:T(1024)(128)(2,1)S(1)}, bf16[1152]{0:T(1024)(128)(2,1)S(1)}, bf16[1152]{0:T(1024)(128)(2,1)S...) all-reduce(bf16[1152]{0:T(1024)(128)(2,1)S(1)} %dynamic-update-slic, ...), channel_id=1, replica_groups=mesh['dp'=8,'tensor'=4] {'dp'}, use_global_device_ids=true, to_apply=%add.6 | all-reduce | flops 13520 | bytes 54080
  51.9 8.4 %collective-permute-done = bf16[1,184,1152]{2,1,0:T(8,128)(2,1)S(1)} collective-permute-done((bf16[1,184,1152]{2,1,0:T(8,128)(2,1)S(1)}, bf16[1,184,1152]{2,1,0:T(8,128)(2,1)S(1)}, u32[]{:S(2)}, u32[]{:S(2)}) %collective-permute-start) | collective-permute-done | bytes 423968 | tf_op jit(solution)/shard_map/ppermute | solution.py:27
  60.6 11.1 %all_gather.55 = bf16[1152,288]{1,0:T(8,128)(2,1)S(1)} all-gather(bf16[144,288]{1,0:T(8,128)(2,1)S(1)} %copy-done.22), channel_id=1, replica_groups=mesh['dp'=8,'tensor'=4] {'dp'}, dimensions={0}, use_global_device_ids=true | all-gather | bytes 746496 | tf_op jit(solution)/shard_map/all_gather | solution.py:140
  71.7 10.7 %all_gather.57 = bf16[1152,288]{1,0:T(8,128)(2,1)S(1)} all-gather(bf16[144,288]{1,0:T(8,128)(2,1)S(1)} %copy-done.23), channel_id=1, replica_groups=mesh['dp'=8,'tensor'=4] {'dp'}, dimensions={0}, use_global_device_ids=true | all-gather | bytes 746496 | tf_op jit(solution)/shard_map/all_gather | solution.py:141
  82.4 10.0 %all_gather.53 = bf16[1152,288]{1,0:T(8,128)(2,1)S(1)} all-gather(bf16[144,288]{1,0:T(8,128)(2,1)S(1)} %copy-done.24), channel_id=1, replica_groups=mesh['dp'=8,'tensor'=4] {'dp'}, dimensions={0}, use_global_device_ids=true | all-gather | bytes 746496 | tf_op jit(solution)/shard_map/all_gather | solution.py:142
  92.4 11.0 %all_gather.58 = bf16[288,1152]{0,1:T(8,128)(2,1)S(1)} all-gather(bf16[288,144]{0,1:T(8,128)(2,1)S(1)} %copy-done.25), channel_id=1, replica_groups=mesh['dp'=8,'tensor'=4] {'dp'}, dimensions={1}, use_global_device_ids=true | all-gather | bytes 746496 | tf_op jit(solution)/shard_map/all_gather | solution.py:143
  103.5 6.5 fusion.32
  117.0 12.8 %convolution_convert_fusion.4 = bf16[4,72,736]{2,1,0:T(8,128)(2,1)S(1)} fusion(bf16[736,4,72]{0,2,1:T(8,128)(2,1)S(1)} %bitcast.107, f32[4,736,736]{1,2,0:T(8,128)S(1)} %get-tuple-element.107, f32[4,736]{1,0:T(4,128)S(1)} %log_add_fusion, pred[736]{0:T(1024)(128)(4,1)S(1)} %compare_reduce_fusion), kind=kOutput, calls=%fused_computation.89 | convolution fusion | flops 318729216 | bytes 9527520 | tf_op jit(solution)/shard_map/while/body/eval_jaxpr/hqk,khd->qhd/dot_general | solution.py:83
  137.2 39.1 %reduce-scatter.35.cloned.1.call-done = bf16[1,184,1152]{2,1,0:T(8,128)(2,1)} async-done(((bf16[1,736,1152]{2,1,0:T(8,128)(2,1)}), bf16[1,184,1152]{2,1,0:T(8,128)(2,1)}) %reduce-scatter.35.cloned.1.call-update) | async-done | bytes 423952
  184.5 9.2 %collective-permute-done.2 = bf16[1,184,1152]{2,1,0:T(8,128)(2,1)S(1)} collective-permute-done((bf16[1,184,1152]{2,1,0:T(8,128)(2,1)S(1)}, bf16[1,184,1152]{2,1,0:T(8,128)(2,1)S(1)}, u32[]{:S(2)}, u32[]{:S(2)}) %collective-permute-start.2) | collective-permute-done | bytes 423968 | tf_op jit(solution)/shard_map/ppermute | solution.py:27
  196.4 52.1 %collective-permute-done.5 = bf16[1,368,1152]{2,1,0:T(8,128)(2,1)} collective-permute-done((bf16[1,368,1152]{2,1,0:T(8,128)(2,1)}, bf16[1,368,1152]{2,1,0:T(8,128)(2,1)}, u32[]{:S(2)}, u32[]{:S(2)}) %collective-permute-start.5) | collective-permute-done | bytes 847904 | tf_op jit(solution)/shard_map/ppermute | solution.py:27
  248.6 7.4 fusion.20
  256.0 9.9 %collective-permute-done.3 = bf16[1,368,1152]{2,1,0:T(8,128)(2,1)} collective-permute-done((bf16[1,368,1152]{2,1,0:T(8,128)(2,1)}, bf16[1,368,1152]{2,1,0:T(8,128)(2,1)}, u32[]{:S(2)}, u32[]{:S(2)}) %collective-permute-start.3) | collective-permute-done | bytes 847904 | tf_op jit(solution)/shard_map/ppermute | solution.py:27
  265.9 7.4 fusion.26
  273.3 6.8 convolution_add_fusion.2
  280.1 8.2 %fusion.72 = (f32[1076]{0:T(1024)}, bf16[736,1076]{0,1:T(8,128)(2,1)S(1)}) fusion(f32[736,1076]{0,1:T(8,128)} %convolution_add_fusion.2, bf16[736,1152]{1,0:T(8,128)(2,1)} %fusion.20, bf16[1076,1152]{0,1:T(8,128)(2,1)} %all-gather.5.cloned.1.call-done), kind=kOutput, calls=%fused_computation.149 | convolution fusion | flops 1840458240 | bytes 8930768 | tf_op jit(solution)/shard_map/dot_general | solution.py:63
  293.6 7.2 fusion.7
  301.0 30.5 %reduce-scatter.39.cloned.1.call-done = bf16[1,184,1152]{2,1,0:T(8,128)(2,1)} async-done(((bf16[1,736,1152]{2,1,0:T(8,128)(2,1)}), bf16[1,184,1152]{2,1,0:T(8,128)(2,1)}) %reduce-scatter.39.cloned.1.call-update) | async-done | bytes 423952
  333.7 36.9 %reduce-scatter.37.cloned.1.call-done = bf16[1,184,1152]{2,1,0:T(8,128)(2,1)} async-done(((bf16[1,736,1152]{2,1,0:T(8,128)(2,1)}), bf16[1,184,1152]{2,1,0:T(8,128)(2,1)}) %reduce-scatter.37.cloned.1.call-update) | async-done | bytes 423952
  374.9 9.8 %collective-permute-done.6 = bf16[1,184,1152]{2,1,0:T(8,128)(2,1)S(1)} collective-permute-done((bf16[1,184,1152]{2,1,0:T(8,128)(2,1)S(1)}, bf16[1,184,1152]{2,1,0:T(8,128)(2,1)S(1)}, u32[]{:S(2)}, u32[]{:S(2)}) %collective-permute-start.6) | collective-permute-done | bytes 423968 | tf_op jit(solution)/shard_map/ppermute | solution.py:27
  387.0 36.5 %collective-permute-done.7 = bf16[1,368,1152]{2,1,0:T(8,128)(2,1)S(1)} collective-permute-done((bf16[1,368,1152]{2,1,0:T(8,128)(2,1)S(1)}, bf16[1,368,1152]{2,1,0:T(8,128)(2,1)S(1)}, u32[]{:S(2)}, u32[]{:S(2)}) %collective-permute-start.7) | collective-permute-done | bytes 847904 | tf_op jit(solution)/shard_map/ppermute | solution.py:27
  423.5 6.5 fusion.14
  431.1 5.7 fusion.70
  463.7 7.0 fusion.66
  472.2 6.3 fusion.62
  480.1 6.1 reduce-scatter.41.cloned.1.call-done
  487.7 41.7 %all-reduce.13 = (f32[1152]{0:T(1024)S(1)}, f32[1152]{0:T(1024)S(1)}, f32[1152]{0:T(1024)S(1)}, f32[1152]{0:T(1024)S(1)}, f32[1152]{0:T(1024)S(1)}, /*index=5*/f...) all-reduce(f32[1152]{0:T(1024)S(1)} %get-tuple-element.74, ...), channel_id=1, replica_groups=mesh['dp'=8,'tensor'=4] {'dp','tensor'}, use_global_device_ids=true, to_apply=%region_22.24 | all-reduce | flops 13520 | bytes 108160 | tf_op jit(solution)/shard_map/psum | solution.py:269
  537.4 34.9 %reduce-scatter.27.cloned.1.call-done = f32[144,288]{1,0:T(8,128)} async-done(((f32[1152,288]{1,0:T(8,128)}), f32[144,288]{1,0:T(8,128)}) %reduce-scatter.27.cloned.1.call-update) | async-done | bytes 165904 | tf_op jit(solution)/shard_map/reduce_scatter | solution.py:255
  572.3 43.4 %reduce-scatter.23.cloned.1.call-done = f32[144,288]{1,0:T(8,128)} async-done(((f32[1152,288]{1,0:T(8,128)}), f32[144,288]{1,0:T(8,128)}) %reduce-scatter.23.cloned.1.call-update) | async-done | bytes 165904 | tf_op jit(solution)/shard_map/reduce_scatter | solution.py:253
  615.7 43.4 %reduce-scatter.25.cloned.1.call-done = f32[144,288]{1,0:T(8,128)} async-done(((f32[1152,288]{1,0:T(8,128)}), f32[144,288]{1,0:T(8,128)}) %reduce-scatter.25.cloned.1.call-update) | async-done | bytes 165904 | tf_op jit(solution)/shard_map/reduce_scatter | solution.py:254
  659.1 60.9 %reduce-scatter.33.cloned.1.call-done = f32[1076,144]{0,1:T(8,128)} async-done(((f32[1076,1152]{0,1:T(8,128)}), f32[1076,144]{0,1:T(8,128)}) %reduce-scatter.33.cloned.1.call-update) | async-done | bytes 619792 | tf_op jit(solution)/shard_map/reduce_scatter | solution.py:258
  720.1 61.2 %reduce-scatter.31.cloned.1.call-done = f32[144,1076]{1,0:T(8,128)} async-done(((f32[1152,1076]{1,0:T(8,128)}), f32[144,1076]{1,0:T(8,128)}) %reduce-scatter.31.cloned.1.call-update) | async-done | bytes 619792 | tf_op jit(solution)/shard_map/reduce_scatter | solution.py:257
  (196 shorter events, 96.2 us)
Async XLA Ops:
  8.0 52.6 %copy-start.27 = (s32[1,736]{1,0:T(1,128)S(1)}, s32[1,736]{1,0:T(1,128)}, u32[]{:S(2)}) copy-start(s32[1,736]{1,0:T(1,128)} %param.21) | copy-start | bytes 8836
  8.0 52.6 %copy-start.22 = (bf16[144,288]{1,0:T(8,128)(2,1)S(1)}, bf16[144,288]{1,0:T(8,128)(2,1)}, u32[]{:S(2)}) copy-start(bf16[144,288]{1,0:T(8,128)(2,1)} %param.22) | copy-start | bytes 248836
  8.0 63.7 %copy-start.23 = (bf16[144,288]{1,0:T(8,128)(2,1)S(1)}, bf16[144,288]{1,0:T(8,128)(2,1)}, u32[]{:S(2)}) copy-start(bf16[144,288]{1,0:T(8,128)(2,1)} %param.23) | copy-start | bytes 248836
  8.1 74.4 %copy-start.24 = (bf16[144,288]{1,0:T(8,128)(2,1)S(1)}, bf16[144,288]{1,0:T(8,128)(2,1)}, u32[]{:S(2)}) copy-start(bf16[144,288]{1,0:T(8,128)(2,1)} %param.24) | copy-start | bytes 248836
  8.1 84.3 %copy-start.25 = (bf16[288,144]{0,1:T(8,128)(2,1)S(1)}, bf16[288,144]{0,1:T(8,128)(2,1)}, u32[]{:S(2)}) copy-start(bf16[288,144]{0,1:T(8,128)(2,1)} %param.25) | copy-start | bytes 248836
  8.1 168.2 %reduce-scatter.35.cloned.1.call-start = ((), (), s32[]{:S(2)}) async-start(), calls=%async_computation.18 | async-start | bytes 2119680
  48.2 12.0 %collective-permute-start = (bf16[1,184,1152]{2,1,0:T(8,128)(2,1)S(1)}, bf16[1,184,1152]{2,1,0:T(8,128)(2,1)S(1)}, u32[]{:S(2)}, u32[]{:S(2)}) collective-permute-start(bf16[1,184,1152]{2,1,0:T(8,128)(2,1)S(1)} %fusion.50), channel_id=1, source_target_pairs={{0,3},{1,0},{2,1},{3,2},{4,7},{5,4},{6,5},{7,6},{8,11},{9,8},{10,9... | collective-permute-start | bytes 1271816 | tf_op jit(solution)/shard_map/ppermute | solution.py:27
  60.3 43.1 %collective-permute-start.1 = (bf16[1,368,1152]{2,1,0:T(8,128)(2,1)S(1)}, bf16[1,368,1152]{2,1,0:T(8,128)(2,1)}, u32[]{:S(2)}, u32[]{:S(2)}) collective-permute-start(bf16[1,368,1152]{2,1,0:T(8,128)(2,1)S(1)} %pad_maximum_fusion), channel_id=1, source_target_pairs={{0,2},{1,3},{2,0},{3,1},{4,6},{5,7},{6,4},{7,5},{8,10},{9,11},{10,... | collective-permute-start | bytes 2543624 | tf_op jit(solution)/shard_map/ppermute | solution.py:27
  71.7 39.0 %copy-start.4 = (bf16[1152,288]{1,0:T(8,128)(2,1)}, bf16[1152,288]{1,0:T(8,128)(2,1)S(1)}, u32[]{:S(2)}) copy-start(bf16[1152,288]{1,0:T(8,128)(2,1)S(1)} %all_gather.55) | copy-start | bytes 1990660
  129.8 46.4 %copy-start = (bf16[1,184,1152]{2,1,0:T(8,128)(2,1)S(1)}, bf16[1,184,1152]{2,1,0:T(8,128)(2,1)}, u32[]{:S(2)}) copy-start(bf16[1,184,1152]{2,1,0:T(8,128)(2,1)} %param.20) | copy-start | bytes 1271812
  133.0 140.3 %all-gather.3.cloned.1.call-start = ((), (), s32[]{:S(2)}) async-start(), calls=%async_computation.10 | async-start | bytes 2985984 | tf_op jit(solution)/shard_map/all_gather | solution.py:144
  133.5 146.6 %all-gather.5.cloned.1.call-start = ((), (), s32[]{:S(2)}) async-start(), calls=%async_computation.11 | async-start | bytes 2985984 | tf_op jit(solution)/shard_map/all_gather | solution.py:145
  134.1 197.4 %reduce-scatter.39.cloned.1.call-start = ((), (), s32[]{:S(2)}) async-start(), calls=%async_computation.20 | async-start | bytes 2119680
  134.2 49.3 %collective-permute-start.4 = (bf16[1,184,1152]{2,1,0:T(8,128)(2,1)S(1)}, bf16[1,184,1152]{2,1,0:T(8,128)(2,1)S(1)}, u32[]{:S(2)}, u32[]{:S(2)}) collective-permute-start(bf16[1,184,1152]{2,1,0:T(8,128)(2,1)S(1)} %copy-done.3), channel_id=1, source_target_pairs={{0,3},{1,0},{2,1},{3,2},{4,7},{5,4},{6,5},{7,6},{8,11},{9,8},{10,9... | collective-permute-start | bytes 1271816 | tf_op jit(solution)/shard_map/ppermute | solution.py:27
  180.1 13.6 %collective-permute-start.2 = (bf16[1,184,1152]{2,1,0:T(8,128)(2,1)S(1)}, bf16[1,184,1152]{2,1,0:T(8,128)(2,1)S(1)}, u32[]{:S(2)}, u32[]{:S(2)}) collective-permute-start(bf16[1,184,1152]{2,1,0:T(8,128)(2,1)S(1)} %add_convert_fusion.1), channel_id=1, source_target_pairs={{0,3},{1,0},{2,1},{3,2},{4,7},{5,4},{6,5},{7,6},{8,11},{9,8},{10,9... | collective-permute-start | bytes 1271816 | tf_op jit(solution)/shard_map/ppermute | solution.py:27
  184.5 64.1 %collective-permute-start.5 = (bf16[1,368,1152]{2,1,0:T(8,128)(2,1)}, bf16[1,368,1152]{2,1,0:T(8,128)(2,1)}, u32[]{:S(2)}, u32[]{:S(2)}) collective-permute-start(bf16[1,368,1152]{2,1,0:T(8,128)(2,1)} %pad_maximum_fusion.2), channel_id=1, source_target_pairs={{0,2},{1,3},{2,0},{3,1},{4,6},{5,7},{6,4},{7,5},{8,10},{9,11},{10,... | collective-permute-start | bytes 2543624 | tf_op jit(solution)/shard_map/ppermute | solution.py:27
  195.4 70.5 %collective-permute-start.3 = (bf16[1,368,1152]{2,1,0:T(8,128)(2,1)}, bf16[1,368,1152]{2,1,0:T(8,128)(2,1)}, u32[]{:S(2)}, u32[]{:S(2)}) collective-permute-start(bf16[1,368,1152]{2,1,0:T(8,128)(2,1)} %pad_maximum_fusion.1), channel_id=1, source_target_pairs={{0,2},{1,3},{2,0},{3,1},{4,6},{5,7},{6,4},{7,5},{8,10},{9,11},{10,... | collective-permute-start | bytes 2543624 | tf_op jit(solution)/shard_map/ppermute | solution.py:27
  196.3 69.6 %copy-start.17 = (bf16[1,184,1152]{2,1,0:T(8,128)(2,1)S(1)}, bf16[1,184,1152]{2,1,0:T(8,128)(2,1)}, u32[]{:S(2)}) copy-start(bf16[1,184,1152]{2,1,0:T(8,128)(2,1)} %copy-done.16) | copy-start | bytes 1271812
  293.5 77.1 %reduce-scatter.37.cloned.1.call-start = ((), (), s32[]{:S(2)}) async-start(), calls=%async_computation.19 | async-start | bytes 2119680
  300.8 185.4 %reduce-scatter.41.cloned.1.call-start = ((), (), s32[]{:S(2)}) async-start(), calls=%async_computation.21 | async-start | bytes 2119680
  370.6 66.2 %slice-start = ((s8[9043968]{0:T(1024)(128)(4,1)}), s8[4194304]{0:T(1024)(128)(4,1)S(1)}, s32[]{:S(2)}) async-start(s8[9043968]{0:T(1024)(128)(4,1)} %bitcast.89), calls=%async_computation.22 | async-start | bytes 8388608
  373.3 56.8 %copy-start.19 = (bf16[288,1152]{0,1:T(8,128)(2,1)S(1)}, bf16[288,1152]{0,1:T(8,128)(2,1)}, u32[]{:S(2)}) copy-start(bf16[288,1152]{0,1:T(8,128)(2,1)} %copy-done.18) | copy-start | bytes 1990660
  373.3 11.4 %collective-permute-start.6 = (bf16[1,184,1152]{2,1,0:T(8,128)(2,1)S(1)}, bf16[1,184,1152]{2,1,0:T(8,128)(2,1)S(1)}, u32[]{:S(2)}, u32[]{:S(2)}) collective-permute-start(bf16[1,184,1152]{2,1,0:T(8,128)(2,1)S(1)} %convert_element_type.180), channel_id=1, source_target_pairs={{0,3},{1,0},{2,1},{3,2},{4,7},{5,4},{6,5},{7,6},{8,11},{9,8},{10,9... | collective-permute-start | bytes 1271816 | tf_op jit(solution)/shard_map/ppermute | solution.py:27
  384.8 46.1 %copy-start.21 = (bf16[4,72,736]{2,1,0:T(8,128)(2,1)S(1)}, bf16[4,72,736]{2,1,0:T(8,128)(2,1)}, u32[]{:S(2)}) copy-start(bf16[4,72,736]{2,1,0:T(8,128)(2,1)} %copy-done.20) | copy-start | bytes 1271812
  384.8 52.0 %slice-start.1 = ((s8[9043968]{0:T(1024)(128)(4,1)}), s8[4194304]{0:T(1024)(128)(4,1)S(1)}, s32[]{:S(2)}) async-start(s8[9043968]{0:T(1024)(128)(4,1)} %bitcast.89), calls=%async_computation.23 | async-start | bytes 8388608
  384.8 38.7 %collective-permute-start.7 = (bf16[1,368,1152]{2,1,0:T(8,128)(2,1)S(1)}, bf16[1,368,1152]{2,1,0:T(8,128)(2,1)S(1)}, u32[]{:S(2)}, u32[]{:S(2)}) collective-permute-start(bf16[1,368,1152]{2,1,0:T(8,128)(2,1)S(1)} %pad_maximum_fusion.3), channel_id=1, source_target_pairs={{0,2},{1,3},{2,0},{3,1},{4,6},{5,7},{6,4},{7,5},{8,10},{9,11},{10,... | collective-permute-start | bytes 2543624 | tf_op jit(solution)/shard_map/ppermute | solution.py:27
  447.9 89.5 %reduce-scatter.29.cloned.1.call-start = ((), (), s32[]{:S(2)}) async-start(), calls=%async_computation.15 | async-start | bytes 1990656 | tf_op jit(solution)/shard_map/reduce_scatter | solution.py:256
  451.8 120.5 %reduce-scatter.27.cloned.1.call-start = ((), (), s32[]{:S(2)}) async-start(), calls=%async_computation.14 | async-start | bytes 1990656 | tf_op jit(solution)/shard_map/reduce_scatter | solution.py:255
  455.7 160.1 %reduce-scatter.23.cloned.1.call-start = ((), (), s32[]{:S(2)}) async-start(), calls=%async_computation.12 | async-start | bytes 1990656 | tf_op jit(solution)/shard_map/reduce_scatter | solution.py:253
  459.6 199.5 %reduce-scatter.25.cloned.1.call-start = ((), (), s32[]{:S(2)}) async-start(), calls=%async_computation.13 | async-start | bytes 1990656 | tf_op jit(solution)/shard_map/reduce_scatter | solution.py:254
  463.7 256.4 %reduce-scatter.33.cloned.1.call-start = ((), (), s32[]{:S(2)}) async-start(), calls=%async_computation.17 | async-start | bytes 5971968 | tf_op jit(solution)/shard_map/reduce_scatter | solution.py:258
  470.8 310.5 %reduce-scatter.31.cloned.1.call-start = ((), (), s32[]{:S(2)}) async-start(), calls=%async_computation.16 | async-start | bytes 5971968 | tf_op jit(solution)/shard_map/reduce_scatter | solution.py:257
  (23 other events, 156.8 us)
Sparse Core Ops, SparseCore 0:
  133.1 43.1 reduce-scatter.34
  293.6 37.8 reduce-scatter.38
  333.9 36.6 reduce-scatter.36
  448.0 38.0 reduce-scatter.40
  490.0 39.3 reduce-scatter.28
  533.1 39.1 reduce-scatter.26
  576.3 39.4 reduce-scatter.22
  619.7 39.4 reduce-scatter.24
  663.1 56.9 reduce-scatter.32
  724.3 56.9 reduce-scatter.30
Sparse Core Ops, SparseCore 1:
  135.3 30.0 all-gather.2
  167.2 30.1 all-gather.4
